TPU v7x, 32 devices: a whole 2x2x4 slice. The times are simulated.
32 devices in a mesh: sector: 8 (over y, x, core), term: 4 (over z).
Axes of the slice: x: 2, y: 2, z: 4, core: 2. Of those that a mesh axis runs over, the one named last changes fastest.
Arguments:
- x_start: float32 [8, 384, 384], P('sector', 'term'), may hold values from -6 to 6
- x_prev: float32 [8, 384, 384], P('sector', 'term'), may hold values from -6 to 6
- precond: float32 [8, 384, 384], P('sector', 'term'), may hold values from 0.5 to 6
- left_env: bfloat16 [256, 384, 384], P(('sector', 'term')), may hold values from -0.20412415 to 1.2041241
- right_env: bfloat16 [256, 384, 384], P(('sector', 'term')), may hold values from -0.20412415 to 1.2041241
- triples: int32 [640, 4], P(('sector', 'term')), may hold values from 0 to 63, as said below
- trip_count: int32 [8, 4], P('sector', 'term'), may hold values from 5 to 20, as said below
- term_coef: float32 [64], replicated, may hold values from 0.25 to 1
- lanczos_beta: float32 [3], replicated, may hold values from 0.3 to 1.2
- block_owner: int32 [8], replicated, may hold values from 0 to 7, each once
Outputs:
- final_vector: float32 [8, 384, 384], P('sector', 'term')
- rayleigh: float32 [3], replicated
Inputs may be any that keep to these rules, and one draw needn't show every extreme that they name: `triples`: Columns: a left slot below 8, a wavefunction block id below 8, a right slot below 8, an operator term below 64. `trip_count`: some device has exactly 20 live triples in every draw. `block_owner`: each sector index holds exactly one block.
All inputs are finite; a program needn't handle non-finite values.
Results may differ from a plain program's by a relative error of at most 0.006.
Values may be sent and summed in bfloat16 or wider, within the bound.
No kernel may reach another device: no remote copies, remote signals or barrier semaphores. Data moves between devices by JAX's collectives and lax.ppermute only.
A program may use at most 64 MiB of HBM per device.

v0:
```python
import math
import jax
import jax.numpy as jnp
from jax import lax
from jax.sharding import PartitionSpec as P

APPS = 3
EPSILON = 1e-06


def local(
    x_start,
    x_prev,
    precond,
    left_env,
    right_env,
    triples,
    trip_count,
    term_coef,
    lanczos_beta,
    block_owner,
):
    sectors = lax.axis_size("sector")
    term_count = lax.axis_size("term")
    block_size = left_env.shape[1]
    share_rows = x_start.shape[1]
    cell_count = sectors * block_size * block_size
    normaliser = 1.0 / math.sqrt(term_count * triples.shape[0])
    live_count = trip_count[0, 0]
    term_match = triples[:, 3:4] == jnp.arange(term_coef.shape[0], dtype=jnp.int32)[None, :]
    coefficient = jnp.sum(jnp.where(term_match, term_coef[None, :], 0.0), axis=1)
    owner_match = triples[:, 1:2] == jnp.arange(sectors, dtype=jnp.int32)[None, :]
    owner_rows = jnp.sum(jnp.where(owner_match, block_owner[None, :], 0), axis=1)

    def own_rows(array):
        return lax.dynamic_slice_in_dim(array, lax.axis_index("term") * share_rows, share_rows, 1)

    current, previous, diagonal = (
        lax.all_gather(x_start, "term", axis=1, tiled=True),
        lax.all_gather(x_prev, "term", axis=1, tiled=True),
        lax.all_gather(precond, "term", axis=1, tiled=True),
    )
    quotients = []
    for position in range(APPS):
        wave_half = current.astype(jnp.bfloat16)
        gathered = lax.all_gather(wave_half, "sector", axis=0, tiled=True)

        def add_triple(triple, accumulated):
            left_block = lax.dynamic_index_in_dim(left_env, triples[triple, 0], 0, keepdims=False)
            wave_block = lax.dynamic_index_in_dim(gathered, owner_rows[triple], 0, keepdims=False)
            right_block = lax.dynamic_index_in_dim(right_env, triples[triple, 2], 0, keepdims=False)
            middle = jnp.dot(left_block, wave_block, preferred_element_type=jnp.float32).astype(
                jnp.bfloat16
            )
            product = jnp.dot(middle, right_block, preferred_element_type=jnp.float32)
            return accumulated + coefficient[triple] * product

        start_sum = jnp.zeros((block_size, block_size), jnp.float32)
        applied = (lax.fori_loop(0, live_count, add_triple, start_sum) * normaliser)[None]
        applied = lax.psum(applied, "term")
        beta_now = lanczos_beta[position]
        cur_own = own_rows(current)
        app_own = own_rows(applied)
        prev_own = own_rows(previous)
        diag_own = own_rows(diagonal)
        diag_square = diag_own * diag_own
        weighted = diag_square * app_own
        weighted_cur = diag_square * cur_own
        sums_all = lax.psum(
            (
                jnp.sum(cur_own * app_own),
                jnp.sum(cur_own * cur_own),
                jnp.sum(weighted * app_own),
                jnp.sum(weighted * cur_own),
                jnp.sum(weighted * prev_own),
                jnp.sum(weighted_cur * cur_own),
                jnp.sum(weighted_cur * prev_own),
                jnp.sum(diag_square * prev_own * prev_own),
            ),
            ("sector", "term"),
        )
        (
            cross_sum,
            self_sum,
            image_image,
            image_current,
            image_previous,
            current_current,
            current_previous,
            previous_previous,
        ) = sums_all
        quotient = cross_sum / self_sum
        square_sum = (
            image_image
            - 2.0 * quotient * image_current
            - 2.0 * beta_now * image_previous
            + quotient * quotient * current_current
            + 2.0 * quotient * beta_now * current_previous
            + beta_now * beta_now * previous_previous
        )
        residual = applied - quotient * current - beta_now * previous
        scaled = diagonal * residual
        following = scaled / jnp.sqrt(square_sum / cell_count + EPSILON)
        previous, current = (current, following)
        quotients.append(quotient)
    return (own_rows(current), jnp.stack(quotients))


def solution(mesh):
    placed = (
        P("sector", "term", None),
        P("sector", "term", None),
        P("sector", "term", None),
        P(("sector", "term"), None, None),
        P(("sector", "term"), None, None),
        P(("sector", "term"), None),
        P("sector", "term"),
        P(),
        P(),
        P(),
    )
    return jax.shard_map(
        local,
        mesh=mesh,
        in_specs=placed,
        out_specs=(P("sector", "term", None), P()),
        check_vma=False,
    )
```

profile of v0, /device:TPU:0, one launch (start us, length us, event | category | flops | bytes accessed | tf_op | source)
XLA Modules:
  0.0 1039.4 jit_solution(10864611968168883217)
XLA Ops:
  7.2 18.5 %all_gather.19 = f32[1,384,384]{2,1,0:T(8,128)S(1)} all-gather(f32[1,96,384]{2,1,0:T(8,128)} %param.16), channel_id=1, replica_groups=mesh['sector'=8,'term'=4] {'term'}, dimensions={1}, use_global_device_ids=true | all-gather | bytes 737280 | tf_op jit(solution)/shard_map/all_gather | solution.py:39
  25.7 0.8 convert_element_type.18
  26.5 0.8 slice_bitcast_fusion
  27.3 0.8 select_reduce_fusion
  28.1 0.7 select_reduce_fusion.1
  28.9 27.8 %all-gather.4.cloned.1.call-done = bf16[8,384,384]{2,1,0:T(8,128)(2,1)} async-done(((bf16[1,384,384]{2,1,0:T(8,128)(2,1)}), bf16[8,384,384]{2,1,0:T(8,128)(2,1)}) %all-gather.4.cloned.1.call-update) | async-done | bytes 2359312 | tf_op jit(solution)/shard_map/all_gather | solution.py:46
  56.8 105.1 %while.30 = (s32[]{:T(128)}, f32[384,384]{1,0:T(8,128)S(1)}, s32[]{:T(128)}, f32[20]{0:T(128)S(1)}, s32[20,4]{0,1:T(4,128)S(1)}, /*index=5*/bf16[8,384,384]{2,1,...) while((s32[]{:T(128)}, f32[384,384]{1,0:T(8,128)S(1)}, ...), condition=%wide.region_3.4_spmd, body=%wide.region_2.3_spmd.sunk | while | flops 226934800 | bytes 2065213 | solution.py:59
  64.8 2.4 fusion.58
  75.3 2.4 fusion.58
  85.7 2.4 fusion.58
  96.1 2.4 fusion.58
  106.6 2.4 fusion.58
  117.0 2.4 fusion.58
  127.5 2.4 fusion.58
  137.9 2.4 fusion.58
  148.4 2.4 fusion.58
  158.8 2.4 fusion.58
  161.9 0.9 multiply_bitcast_fusion.2
  165.4 33.6 %all_gather.18 = f32[1,384,384]{2,1,0:T(8,128)S(1)} all-gather(f32[1,96,384]{2,1,0:T(8,128)S(1)} %copy-done), channel_id=1, replica_groups=mesh['sector'=8,'term'=4] {'term'}, dimensions={1}, use_global_device_ids=true | all-gather | bytes 737280 | tf_op jit(solution)/shard_map/all_gather | solution.py:41
  199.0 16.4 %all_gather.21 = f32[1,384,384]{2,1,0:T(8,128)S(1)} all-gather(f32[1,96,384]{2,1,0:T(8,128)S(1)} %copy-done.1), channel_id=1, replica_groups=mesh['sector'=8,'term'=4] {'term'}, dimensions={1}, use_global_device_ids=true | all-gather | bytes 737280 | tf_op jit(solution)/shard_map/all_gather | solution.py:40
  215.4 97.2 %all-reduce.7.cloned.1.call-done = f32[1,384,384]{2,1,0:T(8,128)} async-done(((f32[1,384,384]{2,1,0:T(8,128)}), f32[1,384,384]{2,1,0:T(8,128)}) %all-reduce.7.cloned.1.call-update) | async-done | bytes 589840 | tf_op jit(solution)/shard_map/psum | solution.py:60
  312.6 1.7 fusion.39
  314.3 42.7 %all-reduce.2 = (f32[]{:T(128)}, f32[]{:T(128)}, f32[]{:T(128)}, f32[]{:T(128)}, f32[]{:T(128)}, /*index=5*/f32[]{:T(128)}, f32[]{:T(128)}, f32[]{:T(128)}) all-reduce(f32[]{:T(128)} %get-tuple-element.167, f32[]{:T(128)} %get-tuple-element.166, f32[]{:T(128)} %get-tuple-element.168, ...), channel_id=1, replica_groups=mesh['sector'=8,'term'=4] {'sector','term'}, use_global_device_ids=true, to_apply=%region_10.11 | all-reduce | flops 8 | bytes 64 | tf_op jit(solution)/shard_map/psum | solution.py:69
  362.8 2.5 fusion.41
  365.4 29.6 %all-gather.6.cloned.1.call-done = bf16[8,384,384]{2,1,0:T(8,128)(2,1)} async-done(((bf16[1,384,384]{2,1,0:T(8,128)(2,1)}), bf16[8,384,384]{2,1,0:T(8,128)(2,1)}) %all-gather.6.cloned.1.call-update) | async-done | bytes 2359312 | tf_op jit(solution)/shard_map/all_gather | solution.py:46
  395.1 105.1 %while.31 = (s32[]{:T(128)}, f32[384,384]{1,0:T(8,128)S(1)}, s32[]{:T(128)}, f32[20]{0:T(128)S(1)}, s32[20,4]{0,1:T(4,128)S(1)}, /*index=5*/bf16[8,384,384]{2,1,...) while((s32[]{:T(128)}, f32[384,384]{1,0:T(8,128)S(1)}, ...), condition=%wide.region_22.23_spmd, body=%wide.region_21.22_spmd.sunk | while | flops 226934800 | bytes 2065213 | solution.py:59
  403.1 2.4 fusion.62
  413.5 2.4 fusion.62
  423.9 2.4 fusion.62
  434.4 2.4 fusion.62
  444.8 2.4 fusion.62
  455.3 2.4 fusion.62
  465.7 2.4 fusion.62
  476.2 2.4 fusion.62
  486.6 2.4 fusion.62
  497.0 2.4 fusion.62
  500.1 0.9 multiply_bitcast_fusion.1
  503.8 140.3 %all-reduce.9.cloned.1.call-done = f32[1,384,384]{2,1,0:T(8,128)} async-done(((f32[1,384,384]{2,1,0:T(8,128)}), f32[1,384,384]{2,1,0:T(8,128)}) %all-reduce.9.cloned.1.call-update) | async-done | bytes 589840 | tf_op jit(solution)/shard_map/psum | solution.py:60
  644.1 1.7 multiply_reduce_fusion.7
  645.8 40.3 %all-reduce.1 = (f32[]{:T(128)}, f32[]{:T(128)}, f32[]{:T(128)}, f32[]{:T(128)}, f32[]{:T(128)}, /*index=5*/f32[]{:T(128)}, f32[]{:T(128)}) all-reduce(f32[]{:T(128)} %get-tuple-element.159, f32[]{:T(128)} %get-tuple-element.160, f32[]{:T(128)} %get-tuple-element.170, ...), channel_id=1, replica_groups=mesh['sector'=8,'term'=4] {'sector','term'}, use_global_device_ids=true, to_apply=%region_29.30 | all-reduce | flops 7 | bytes 56 | tf_op jit(solution)/shard_map/psum | solution.py:69
  691.3 2.6 fusion.40
  694.0 28.5 %all-gather.8.cloned.1.call-done = bf16[8,384,384]{2,1,0:T(8,128)(2,1)} async-done(((bf16[1,384,384]{2,1,0:T(8,128)(2,1)}), bf16[8,384,384]{2,1,0:T(8,128)(2,1)}) %all-gather.8.cloned.1.call-update) | async-done | bytes 2359312 | tf_op jit(solution)/shard_map/all_gather | solution.py:46
  722.5 110.6 %while.32 = (s32[]{:T(128)}, f32[384,384]{1,0:T(8,128)S(1)}, s32[]{:T(128)}, f32[20]{0:T(128)S(1)}, s32[20,4]{0,1:T(4,128)S(1)}, /*index=5*/bf16[8,384,384]{2,1,...) while((s32[]{:T(128)}, f32[384,384]{1,0:T(8,128)S(1)}, ...), condition=%wide.region_39.40_spmd, body=%wide.region_38.39_spmd.sunk | while | flops 226934800 | bytes 2065213 | solution.py:59
  727.6 0.7 dynamic_slice.282
  731.0 2.5 fusion.66
  738.6 0.7 dynamic_slice.282
  742.0 2.5 fusion.66
  752.3 0.7 dynamic_slice.283
  753.0 2.5 fusion.66
  764.0 2.5 fusion.66
  771.6 0.7 dynamic_slice.282
  775.0 2.5 fusion.66
  782.6 0.7 dynamic_slice.282
  786.0 2.5 fusion.66
  796.3 0.7 dynamic_slice.283
  797.0 2.5 fusion.66
  808.0 2.5 fusion.66
  819.0 2.5 fusion.66
  830.0 2.5 fusion.66
  833.1 0.9 multiply_bitcast_fusion
  836.4 146.3 %all-reduce.11.cloned.1.call-done = f32[1,384,384]{2,1,0:T(8,128)} async-done(((f32[1,384,384]{2,1,0:T(8,128)}), f32[1,384,384]{2,1,0:T(8,128)}) %all-reduce.11.cloned.1.call-update) | async-done | bytes 589840 | tf_op jit(solution)/shard_map/psum | solution.py:60
  982.7 1.7 multiply_reduce_fusion
  984.3 40.3 %all-reduce = (f32[]{:T(128)}, f32[]{:T(128)}, f32[]{:T(128)}, f32[]{:T(128)}, f32[]{:T(128)}, /*index=5*/f32[]{:T(128)}, f32[]{:T(128)}) all-reduce(f32[]{:T(128)} %get-tuple-element.152, f32[]{:T(128)} %get-tuple-element.153, f32[]{:T(128)} %get-tuple-element.169, ...), channel_id=1, replica_groups=mesh['sector'=8,'term'=4] {'sector','term'}, use_global_device_ids=true, to_apply=%region_46.47 | all-reduce | flops 7 | bytes 56 | tf_op jit(solution)/shard_map/psum | solution.py:69
  1030.3 2.2 multiply_divide_fusion.2
  (109 shorter events, 53.0 us)
Async XLA Ops:
  7.2 49.6 %copy-start.2 = (s32[20,4]{0,1:T(4,128)S(1)}, s32[20,4]{0,1:T(4,128)}, u32[]{:S(2)}) copy-start(s32[20,4]{0,1:T(4,128)} %param.21) | copy-start | bytes 964
  7.2 49.5 %all-gather.4.cloned.1.call-start = ((), (), s32[]{:S(2)}) async-start(), calls=%async_computation | async-start | bytes 2654208 | tf_op jit(solution)/shard_map/all_gather | solution.py:46
  26.5 286.1 %all-reduce.7.cloned.1.call-start = ((), (), s32[]{:S(2)}) async-start(), calls=%async_computation.1 | async-start | bytes 1179648 | tf_op jit(solution)/shard_map/psum | solution.py:60
  56.8 106.1 %copy-start.3 = (f32[3]{0:T(128)S(1)}, f32[3]{0:T(128)}, u32[]{:S(2)}) copy-start(f32[3]{0:T(128)} %param.24) | copy-start | bytes 40
  56.8 108.6 %copy-start = (f32[1,96,384]{2,1,0:T(8,128)S(1)}, f32[1,96,384]{2,1,0:T(8,128)}, u32[]{:S(2)}) copy-start(f32[1,96,384]{2,1,0:T(8,128)} %param.18) | copy-start | bytes 442372
  161.9 37.1 %copy-start.1 = (f32[1,96,384]{2,1,0:T(8,128)S(1)}, f32[1,96,384]{2,1,0:T(8,128)}, u32[]{:S(2)}) copy-start(f32[1,96,384]{2,1,0:T(8,128)} %param.17) | copy-start | bytes 442372
  162.8 232.2 %all-gather.6.cloned.1.call-start = ((), (), s32[]{:S(2)}) async-start(), calls=%async_computation.2 | async-start | bytes 2654208 | tf_op jit(solution)/shard_map/all_gather | solution.py:46
  365.3 278.8 %all-reduce.9.cloned.1.call-start = ((), (), s32[]{:S(2)}) async-start(), calls=%async_computation.3 | async-start | bytes 1179648 | tf_op jit(solution)/shard_map/psum | solution.py:60
  501.0 221.4 %all-gather.8.cloned.1.call-start = ((), (), s32[]{:S(2)}) async-start(), calls=%async_computation.4 | async-start | bytes 2654208 | tf_op jit(solution)/shard_map/all_gather | solution.py:46
  693.9 288.7 %all-reduce.11.cloned.1.call-start = ((), (), s32[]{:S(2)}) async-start(), calls=%async_computation.5 | async-start | bytes 1179648 | tf_op jit(solution)/shard_map/psum | solution.py:60
Sparse Core Ops, SparseCore 0:
  26.6 30.0 all-gather.3
  162.9 149.6 all-reduce.6
  365.5 29.5 all-gather.5
  501.1 142.9 all-reduce.8
  694.0 28.3 all-gather.7
  834.1 148.4 all-reduce.10
where the time goes:
time: 1050 us; the launch traced here: 1040 us
  waiting for transfers between devices  470 us (45%)
  blocking collectives  192 us (18%)
  loops' own time  192 us (18%)
  matrix products  73.7 us (7%)
  local copies, waits for them, and re-layouts  56.9 us (5%)
  between operations  37.2 us (4%)
  other arithmetic  17.8 us (2%)
    psum x3, waiting for transfers between devices, local(): applied = lax.psum(applied, 'term')  384 us
    another operation x3, loops' own time, local(): lax.fori_loop(0, live_count, add_triple, start_sum) * normaliser  192 us
    psum x3, blocking collectives, local(): lax.psum((jnp.sum(cur_own * app_own), jnp.sum(cur_own * cur_own), jnp.sum...  123 us
    all_gather x3, waiting for transfers between devices, local(): gathered = lax.all_gather(wave_half, 'sector', axis=0, tiled=True)  86 us
    dot_general x30, matrix products, add_triple(): product = jnp.dot(middle, right_block, preferred_element_type=jnp.float32)  73.7 us
    all_gather x1, blocking collectives, local(): lax.all_gather(precond, 'term', axis=1, tiled=True)  33.6 us
  transfers between devices with their start and end apart: 6, of which 6 were waited for; matrix products, arithmetic and copies ran while one was open for 0% of the time, Pallas kernels for 0%

commit v1 on v0

--- a/solution.py
+++ b/solution.py
@@ -57,7 +57,7 @@
 
         start_sum = jnp.zeros((block_size, block_size), jnp.float32)
         applied = (lax.fori_loop(0, live_count, add_triple, start_sum) * normaliser)[None]
-        applied = lax.psum(applied, "term")
+        applied = jnp.sum(lax.all_gather(applied, "term"), axis=0)
         beta_now = lanczos_beta[position]
         cur_own = own_rows(current)
         app_own = own_rows(applied)

time: 1050 us -> 1060 us (level)
  waiting for transfers between devices: 470 us -> 492 us
    all_gather x0 -> x3, waiting for transfers between devices: none -> 405 us  [local(): applied = jnp.sum(lax.all_gather(applied, 'term'), axis=0)]
    psum x3 -> x0, waiting for transfers between devices: 384 us -> none  [local(): applied = lax.psum(applied, 'term')]
where the time goes in v1:
time: 1060 us; the launch traced here: 1050 us
  waiting for transfers between devices  492 us (46%)
  blocking collectives  194 us (18%)
  loops' own time  185 us (17%)
  matrix products  72.2 us (7%)
  local copies, waits for them, and re-layouts  53.9 us (5%)
  between operations  36.5 us (3%)
  other arithmetic  17.7 us (2%)
    all_gather x3, waiting for transfers between devices, local(): applied = jnp.sum(lax.all_gather(applied, 'term'), axis=0)  405 us
    another operation x3, loops' own time, local(): lax.fori_loop(0, live_count, add_triple, start_sum) * normaliser  185 us
    psum x3, blocking collectives, local(): lax.psum((jnp.sum(cur_own * app_own), jnp.sum(cur_own * cur_own), jnp.sum...  125 us
    all_gather x3, waiting for transfers between devices, local(): gathered = lax.all_gather(wave_half, 'sector', axis=0, tiled=True)  87 us
    dot_general x30, matrix products, add_triple(): product = jnp.dot(middle, right_block, preferred_element_type=jnp.float32)  72.2 us
    all_gather x1, blocking collectives, local(): lax.all_gather(precond, 'term', axis=1, tiled=True)  33.6 us
  transfers between devices with their start and end apart: 6, of which 6 were waited for; matrix products, arithmetic and copies ran while one was open for 0% of the time, Pallas kernels for 0%

profile of v1, /device:TPU:0, one launch (start us, length us, event | category | flops | bytes accessed | tf_op | source)
XLA Modules:
  0.0 1051.2 jit_solution(4836586084209074574)
XLA Ops:
  7.2 18.5 %all_gather.28 = f32[1,384,384]{2,1,0:T(8,128)S(1)} all-gather(f32[1,96,384]{2,1,0:T(8,128)} %param.16), channel_id=1, replica_groups=mesh['sector'=8,'term'=4] {'term'}, dimensions={1}, use_global_device_ids=true | all-gather | bytes 737280 | tf_op jit(solution)/shard_map/all_gather | solution.py:39
  25.7 0.8 convert_element_type.18
  26.5 0.8 slice_bitcast_fusion
  27.3 0.8 select_reduce_fusion
  28.1 0.7 select_reduce_fusion.1
  28.9 27.8 %all-gather.10.cloned.1.call-done = bf16[8,384,384]{2,1,0:T(8,128)(2,1)} async-done(((bf16[1,384,384]{2,1,0:T(8,128)(2,1)}), bf16[8,384,384]{2,1,0:T(8,128)(2,1)}) %all-gather.10.cloned.1.call-update) | async-done | bytes 2359312 | tf_op jit(solution)/shard_map/all_gather | solution.py:46
  56.8 105.1 %while.30 = (s32[]{:T(128)}, f32[384,384]{1,0:T(8,128)S(1)}, s32[]{:T(128)}, f32[20]{0:T(128)S(1)}, s32[20,4]{0,1:T(4,128)S(1)}, /*index=5*/bf16[8,384,384]{2,1,...) while((s32[]{:T(128)}, f32[384,384]{1,0:T(8,128)S(1)}, ...), condition=%wide.region_3.4_spmd, body=%wide.region_2.3_spmd.sunk | while | flops 226934800 | bytes 2065213 | solution.py:59
  64.8 2.4 fusion.75
  75.3 2.4 fusion.75
  85.7 2.4 fusion.75
  96.1 2.4 fusion.75
  106.6 2.4 fusion.75
  117.0 2.4 fusion.75
  127.5 2.4 fusion.75
  137.9 2.4 fusion.75
  148.4 2.4 fusion.75
  158.8 2.4 fusion.75
  161.9 0.9 broadcast_multiply_fusion.2
  165.3 33.6 %all_gather.27 = f32[1,384,384]{2,1,0:T(8,128)S(1)} all-gather(f32[1,96,384]{2,1,0:T(8,128)S(1)} %copy-done), channel_id=1, replica_groups=mesh['sector'=8,'term'=4] {'term'}, dimensions={1}, use_global_device_ids=true | all-gather | bytes 737280 | tf_op jit(solution)/shard_map/all_gather | solution.py:41
  198.9 16.4 %all_gather.31 = f32[1,384,384]{2,1,0:T(8,128)S(1)} all-gather(f32[1,96,384]{2,1,0:T(8,128)S(1)} %copy-done.1), channel_id=1, replica_groups=mesh['sector'=8,'term'=4] {'term'}, dimensions={1}, use_global_device_ids=true | all-gather | bytes 737280 | tf_op jit(solution)/shard_map/all_gather | solution.py:40
  215.3 108.0 %all-gather.16.cloned.1.call-done = f32[1536,384]{1,0:T(8,128)} async-done(((f32[384,384]{1,0:T(8,128)}), f32[1536,384]{1,0:T(8,128)}) %all-gather.16.cloned.1.call-update) | async-done | bytes 2359312 | tf_op jit(solution)/shard_map/all_gather | solution.py:60
  323.4 1.9 reduce.3
  325.2 0.8 fusion.45
  326.0 46.6 %all-reduce.2 = (f32[]{:T(128)}, f32[]{:T(128)}, f32[]{:T(128)}, f32[]{:T(128)}, f32[]{:T(128)}, /*index=5*/f32[]{:T(128)}, f32[]{:T(128)}, f32[]{:T(128)}) all-reduce(f32[]{:T(128)} %get-tuple-element.167, f32[]{:T(128)} %get-tuple-element.166, f32[]{:T(128)} %get-tuple-element.168, ...), channel_id=1, replica_groups=mesh['sector'=8,'term'=4] {'sector','term'}, use_global_device_ids=true, to_apply=%region_10.11 | all-reduce | flops 8 | bytes 64 | tf_op jit(solution)/shard_map/psum | solution.py:69
  378.4 1.5 fusion.57
  379.9 30.2 %all-gather.12.cloned.1.call-done = bf16[8,384,384]{2,1,0:T(8,128)(2,1)} async-done(((bf16[1,384,384]{2,1,0:T(8,128)(2,1)}), bf16[8,384,384]{2,1,0:T(8,128)(2,1)}) %all-gather.12.cloned.1.call-update) | async-done | bytes 2359312 | tf_op jit(solution)/shard_map/all_gather | solution.py:46
  410.2 107.1 %while.31 = (s32[]{:T(128)}, f32[384,384]{1,0:T(8,128)S(1)}, s32[]{:T(128)}, f32[20]{0:T(128)S(1)}, s32[20,4]{0,1:T(4,128)S(1)}, /*index=5*/bf16[8,384,384]{2,1,...) while((s32[]{:T(128)}, f32[384,384]{1,0:T(8,128)S(1)}, ...), condition=%wide.region_22.23_spmd, body=%wide.region_21.22_spmd.sunk | while | flops 226934800 | bytes 2065213 | solution.py:59
  410.9 0.6 constant_dynamic-slice_fusion.10
  418.4 2.4 fusion.79
  421.5 0.6 constant_dynamic-slice_fusion.10
  429.1 2.4 fusion.79
  439.7 2.4 fusion.79
  450.4 2.4 fusion.79
  461.0 2.4 fusion.79
  471.6 2.4 fusion.79
  482.3 2.4 fusion.79
  492.9 2.4 fusion.79
  496.0 0.6 constant_dynamic-slice_fusion.10
  503.6 2.4 fusion.79
  514.2 2.4 fusion.79
  517.3 0.9 broadcast_multiply_fusion.1
  520.5 153.1 %all-gather.18.cloned.1.call-done = f32[1536,384]{1,0:T(8,128)} async-done(((f32[384,384]{1,0:T(8,128)}), f32[1536,384]{1,0:T(8,128)}) %all-gather.18.cloned.1.call-update) | async-done | bytes 2359312 | tf_op jit(solution)/shard_map/all_gather | solution.py:60
  673.7 1.9 reduce.4
  675.5 0.8 multiply_reduce_fusion.5
  676.3 39.4 %all-reduce.1 = (f32[]{:T(128)}, f32[]{:T(128)}, f32[]{:T(128)}, f32[]{:T(128)}, f32[]{:T(128)}, /*index=5*/f32[]{:T(128)}, f32[]{:T(128)}) all-reduce(f32[]{:T(128)} %get-tuple-element.159, f32[]{:T(128)} %get-tuple-element.160, f32[]{:T(128)} %get-tuple-element.170, ...), channel_id=1, replica_groups=mesh['sector'=8,'term'=4] {'sector','term'}, use_global_device_ids=true, to_apply=%region_29.30 | all-reduce | flops 7 | bytes 56 | tf_op jit(solution)/shard_map/psum | solution.py:69
  720.8 1.4 fusion.55
  722.3 29.0 %all-gather.14.cloned.1.call-done = bf16[8,384,384]{2,1,0:T(8,128)(2,1)} async-done(((bf16[1,384,384]{2,1,0:T(8,128)(2,1)}), bf16[8,384,384]{2,1,0:T(8,128)(2,1)}) %all-gather.14.cloned.1.call-update) | async-done | bytes 2359312 | tf_op jit(solution)/shard_map/all_gather | solution.py:46
  751.3 97.4 %while.32 = (s32[]{:T(128)}, f32[384,384]{1,0:T(8,128)S(1)}, s32[]{:T(128)}, f32[20]{0:T(128)S(1)}, s32[20,4]{0,1:T(4,128)S(1)}, /*index=5*/bf16[8,384,384]{2,1,...) while((s32[]{:T(128)}, f32[384,384]{1,0:T(8,128)S(1)}, ...), condition=%wide.region_39.40_spmd, body=%wide.region_38.39_spmd.sunk | while | flops 226934800 | bytes 2065213 | solution.py:59
  758.6 2.3 fusion.83
  768.3 2.3 fusion.83
  778.0 2.3 fusion.83
  787.7 2.3 fusion.83
  797.3 2.3 fusion.83
  807.0 2.3 fusion.83
  816.7 2.3 fusion.83
  826.4 2.3 fusion.83
  836.0 2.3 fusion.83
  845.7 2.3 fusion.83
  848.7 0.9 broadcast_multiply_fusion
  852.0 143.5 %all-gather.20.cloned.1.call-done = f32[1536,384]{1,0:T(8,128)} async-done(((f32[384,384]{1,0:T(8,128)}), f32[1536,384]{1,0:T(8,128)}) %all-gather.20.cloned.1.call-update) | async-done | bytes 2359312 | tf_op jit(solution)/shard_map/all_gather | solution.py:60
  995.4 1.9 reduce.5
  997.3 0.8 multiply_reduce_fusion
  998.1 39.4 %all-reduce = (f32[]{:T(128)}, f32[]{:T(128)}, f32[]{:T(128)}, f32[]{:T(128)}, f32[]{:T(128)}, /*index=5*/f32[]{:T(128)}, f32[]{:T(128)}) all-reduce(f32[]{:T(128)} %get-tuple-element.152, f32[]{:T(128)} %get-tuple-element.153, f32[]{:T(128)} %get-tuple-element.169, ...), channel_id=1, replica_groups=mesh['sector'=8,'term'=4] {'sector','term'}, use_global_device_ids=true, to_apply=%region_46.47 | all-reduce | flops 7 | bytes 56 | tf_op jit(solution)/shard_map/psum | solution.py:69
  1042.5 1.3 fusion.48
  (112 shorter events, 52.3 us)
Async XLA Ops:
  7.2 49.6 %copy-start.2 = (s32[20,4]{0,1:T(4,128)S(1)}, s32[20,4]{0,1:T(4,128)}, u32[]{:S(2)}) copy-start(s32[20,4]{0,1:T(4,128)} %param.21) | copy-start | bytes 964
  7.2 49.5 %all-gather.10.cloned.1.call-start = ((), (), s32[]{:S(2)}) async-start(), calls=%async_computation | async-start | bytes 2654208 | tf_op jit(solution)/shard_map/all_gather | solution.py:46
  26.5 296.9 %all-gather.16.cloned.1.call-start = ((), (), s32[]{:S(2)}) async-start(), calls=%async_computation.3 | async-start | bytes 2949120 | tf_op jit(solution)/shard_map/all_gather | solution.py:60
  56.8 106.1 %copy-start.3 = (f32[3]{0:T(128)S(1)}, f32[3]{0:T(128)}, u32[]{:S(2)}) copy-start(f32[3]{0:T(128)} %param.24) | copy-start | bytes 40
  56.8 108.6 %copy-start = (f32[1,96,384]{2,1,0:T(8,128)S(1)}, f32[1,96,384]{2,1,0:T(8,128)}, u32[]{:S(2)}) copy-start(f32[1,96,384]{2,1,0:T(8,128)} %param.18) | copy-start | bytes 442372
  161.9 37.0 %copy-start.1 = (f32[1,96,384]{2,1,0:T(8,128)S(1)}, f32[1,96,384]{2,1,0:T(8,128)}, u32[]{:S(2)}) copy-start(f32[1,96,384]{2,1,0:T(8,128)} %param.17) | copy-start | bytes 442372
  162.8 247.4 %all-gather.12.cloned.1.call-start = ((), (), s32[]{:S(2)}) async-start(), calls=%async_computation.1 | async-start | bytes 2654208 | tf_op jit(solution)/shard_map/all_gather | solution.py:46
  379.9 293.8 %all-gather.18.cloned.1.call-start = ((), (), s32[]{:S(2)}) async-start(), calls=%async_computation.4 | async-start | bytes 2949120 | tf_op jit(solution)/shard_map/all_gather | solution.py:60
  518.2 233.0 %all-gather.14.cloned.1.call-start = ((), (), s32[]{:S(2)}) async-start(), calls=%async_computation.2 | async-start | bytes 2654208 | tf_op jit(solution)/shard_map/all_gather | solution.py:46
  722.2 273.2 %all-gather.20.cloned.1.call-start = ((), (), s32[]{:S(2)}) async-start(), calls=%async_computation.5 | async-start | bytes 2949120 | tf_op jit(solution)/shard_map/all_gather | solution.py:60
Sparse Core Ops, SparseCore 0:
  26.6 30.0 all-gather.9
  162.9 160.3 all-gather.15
  380.0 30.1 all-gather.11
  518.3 155.2 all-gather.17
  722.4 28.8 all-gather.13
  849.8 145.6 all-gather.19
